TPU v7x, 128 devices: a whole 4x4x4 slice. The times are simulated.
128 devices in a mesh: dp: 8 (over z_hi, x), ctx: 16 (over z_lo, y, core).
Axes of the slice: x: 4, y: 4, z: 4 (z_hi: 2, z_lo: 2; z = z_hi * 2 + z_lo), core: 2. Of those that a mesh axis runs over, the one named last changes fastest.
Arguments:
- resid: bfloat16 [16384, 4096], P(('dp', 'ctx')), may hold values from -6 to 6
- query: bfloat16 [16384, 2048], P(('dp', 'ctx')), may hold values from -40 to 40
- keys: bfloat16 [16384, 512], P(('dp', 'ctx')), may hold values from -40 to 40
- values: bfloat16 [16384, 512], P(('dp', 'ctx')), may hold values from -6 to 6
- doc_lengths: int32 [16], replicated, may hold values from 1 to 2048, 16384 in all
- w_out: bfloat16 [2048, 4096], P('dp'), may hold values from -0.125 to 0.125
- norm_gain: float32 [4096], replicated, may hold values from 0.1 to 1.9
- w_gate: bfloat16 [4096, 7168], P(None, 'dp'), may hold values from -0.09375 to 0.09375
- w_up: bfloat16 [4096, 7168], P(None, 'dp'), may hold values from -0.09375 to 0.09375
- w_down: bfloat16 [7168, 4096], P('dp'), may hold values from -0.0625 to 0.0625
Outputs:
- layer_out: bfloat16 [16384, 4096], P(('dp', 'ctx'))
Inputs may be any that keep to these rules, and one draw needn't show every extreme that they name: `doc_lengths`: the lengths sum to 16384, and the longest is exactly 2048.
All inputs are finite; a program needn't handle non-finite values.
Results may differ from a plain program's by a relative error of at most 0.015.
Values may be sent and summed in bfloat16 or wider, within the bound.
A program may use at most 192 MiB of HBM per device.

v0:
```python
import math
import jax
import jax.numpy as jnp
from jax import lax
from jax.sharding import PartitionSpec as P

HEAD_DIM = 128
ROPE_BASE = 500000.0
EPS = 1e-05
NEG_FILL = -1e30


def from_behind(block, axis, distance):
    devices = range(lax.axis_size(axis))
    route = [(i - distance, i) for i in devices if i - distance in devices]
    return lax.ppermute(block, axis, route)


def rope_tables(rel_pos, head_dim):
    half_dim = head_dim // 2
    freq_index = jnp.arange(half_dim, dtype=jnp.float32)
    inv_freq = jnp.exp(freq_index * (-2.0 * math.log(ROPE_BASE) / head_dim))
    angles = rel_pos.astype(jnp.float32)[:, None] * inv_freq[None, :]
    return (jnp.cos(angles), jnp.sin(angles))


def rotate(field, cosine, sine_val, num_heads, head_dim):
    row_count = field.shape[0]
    half_dim = head_dim // 2
    shaped = field.astype(jnp.float32).reshape(row_count, num_heads, head_dim)
    first_half = shaped[..., :half_dim]
    second_half = shaped[..., half_dim:]
    cos_b = cosine[:, None, :]
    sin_b = sine_val[:, None, :]
    turned = jnp.concatenate(
        [first_half * cos_b - second_half * sin_b, second_half * cos_b + first_half * sin_b],
        axis=-1,
    )
    return turned.reshape(row_count, num_heads * head_dim).astype(jnp.bfloat16)


def doc_starts(doc_lengths, positions):
    doc_ends = jnp.cumsum(doc_lengths)
    starts = doc_ends - doc_lengths
    inside = starts[None, :] <= positions[:, None]
    return jnp.max(jnp.where(inside, starts[None, :], 0), axis=1)


def online_update(
    softmax_state, q_group, key_rows, value_rows, key_pos, query_pos, query_start, score_scale
):
    row_max, row_sum, weighted = softmax_state
    kv_heads = q_group.shape[0]
    head_dim = q_group.shape[2]
    key_heads = key_rows.reshape(key_rows.shape[0], kv_heads, head_dim).transpose(1, 0, 2)
    value_heads = value_rows.reshape(value_rows.shape[0], kv_heads, head_dim).transpose(1, 0, 2)
    scores = (
        jnp.einsum("aqd,akd->aqk", q_group, key_heads, preferred_element_type=jnp.float32)
        * score_scale
    )
    allowed = (key_pos[None, :] >= query_start[:, None]) & (key_pos[None, :] <= query_pos[:, None])
    group_size = q_group.shape[1] // query_pos.shape[0]
    allowed = jnp.tile(allowed, (group_size, 1))[None]
    scores = jnp.where(allowed, scores, NEG_FILL)
    new_max = jnp.maximum(row_max, jnp.max(scores, axis=-1))
    weights = jnp.where(allowed, jnp.exp(scores - new_max[..., None]), 0.0)
    factor = jnp.exp(row_max - new_max)
    row_sum = row_sum * factor + jnp.sum(weights, axis=-1)
    weighted = weighted * factor[..., None] + jnp.einsum(
        "aqk,akd->aqd",
        weights.astype(jnp.bfloat16),
        value_heads,
        preferred_element_type=jnp.float32,
    )
    return (new_max, row_sum, weighted)


def per_device(resid, query, keys, values, doc_lengths, w_out, norm_gain, w_gate, w_up, w_down):
    tok_rows = resid.shape[0]
    dp_count = lax.axis_size("dp")
    ctx_count = lax.axis_size("ctx")
    reach_devs = min(16, dp_count * ctx_count // 4)
    head_dim = HEAD_DIM
    kv_heads = keys.shape[1] // head_dim
    num_heads = query.shape[1] // head_dim
    group_size = num_heads // kv_heads
    my_block = lax.axis_index(("dp", "ctx"))
    local_index = jnp.arange(tok_rows, dtype=jnp.int32)
    query_pos = my_block * tok_rows + local_index
    query_start = doc_starts(doc_lengths, query_pos)
    cosine, sine_val = rope_tables(query_pos - query_start, head_dim)
    q_rot = rotate(query, cosine, sine_val, num_heads, head_dim)
    k_rot = rotate(keys, cosine, sine_val, kv_heads, head_dim)
    q_group = (
        q_rot.reshape(tok_rows, kv_heads, group_size, head_dim)
        .transpose(1, 2, 0, 3)
        .reshape(kv_heads, group_size * tok_rows, head_dim)
    )
    score_scale = 1.0 / math.sqrt(head_dim)
    softmax_state = (
        jnp.full((kv_heads, group_size * tok_rows), NEG_FILL, jnp.float32),
        jnp.zeros((kv_heads, group_size * tok_rows), jnp.float32),
        jnp.zeros((kv_heads, group_size * tok_rows, head_dim), jnp.float32),
    )
    kv_pair = jnp.stack([k_rot, values])
    softmax_state = online_update(
        softmax_state, q_group, k_rot, values, query_pos, query_pos, query_start, score_scale
    )

    def cycle_free_step(turn_index, loop_state):
        inner_state, moving = loop_state
        moving = from_behind(moving, ("dp", "ctx"), 1)
        source = my_block - turn_index - 1
        inner_state = online_update(
            inner_state,
            q_group,
            moving[0],
            moving[1],
            source * tok_rows + local_index,
            query_pos,
            query_start,
            score_scale,
        )
        return (inner_state, moving)

    softmax_state, _ = lax.fori_loop(0, reach_devs, cycle_free_step, (softmax_state, kv_pair))
    row_max, row_sum, weighted = softmax_state
    heads_out = (weighted / row_sum[..., None]).reshape(kv_heads, group_size, tok_rows, head_dim)
    heads_out = (
        heads_out.transpose(2, 0, 1, 3).reshape(tok_rows, num_heads * head_dim).astype(jnp.bfloat16)
    )
    spread = lax.all_to_all(heads_out, "dp", split_axis=1, concat_axis=0, tiled=True)
    projected = lax.psum_scatter(
        jnp.dot(spread, w_out, preferred_element_type=jnp.float32).astype(jnp.bfloat16),
        "dp",
        scatter_dimension=0,
        tiled=True,
    ).astype(jnp.float32)
    residual_sum = resid.astype(jnp.float32) + projected
    mean_sq = jnp.mean(residual_sum * residual_sum, axis=1, keepdims=True)
    normed = (residual_sum * lax.rsqrt(mean_sq + EPS) * norm_gain).astype(jnp.bfloat16)
    piece_rows = lax.all_gather(normed, "dp", axis=0, tiled=True)
    gate_val = jnp.dot(piece_rows, w_gate, preferred_element_type=jnp.float32)
    up_val = jnp.dot(piece_rows, w_up, preferred_element_type=jnp.float32)
    hidden_act = (jax.nn.silu(gate_val) * up_val).astype(jnp.bfloat16)
    partial_rows = jnp.dot(hidden_act, w_down, preferred_element_type=jnp.float32)
    mlp_out = lax.psum_scatter(
        partial_rows.astype(jnp.bfloat16), "dp", scatter_dimension=0, tiled=True
    ).astype(jnp.float32)
    return (residual_sum + mlp_out).astype(jnp.bfloat16)


def solution(mesh):
    return jax.shard_map(
        per_device,
        mesh=mesh,
        in_specs=(
            P(("dp", "ctx"), None),
            P(("dp", "ctx"), None),
            P(("dp", "ctx"), None),
            P(("dp", "ctx"), None),
            P(),
            P("dp", None),
            P(),
            P(None, "dp"),
            P(None, "dp"),
            P("dp", None),
        ),
        out_specs=P(("dp", "ctx"), None),
        check_vma=False,
    )
```

profile of v0, /device:TPU:1, one launch (start us, length us, event | category | flops | bytes accessed | tf_op | source)
XLA Modules:
  0.0 747.8 jit_solution(9612714527674316773)
XLA Ops:
  16.7 258.0 %while.22 = (s32[]{:T(128)}, f32[4,512]{1,0:T(4,128)S(1)}, f32[4,512]{1,0:T(4,128)S(1)}, f32[4,512,128]{2,1,0:T(8,128)S(1)}, bf16[2,128,512]{1,2,0:T(8,128)(2,1)...) while((s32[]{:T(128)}, f32[4,512]{1,0:T(4,128)S(1)}, ...), condition=%wide.region_7.8_spmd.clone, body=%wide.region_4.7_spmd.clone.sunk | while | flops 137154816 | bytes 9210569 | solution.py:126
  16.7 4.6 collective-permute-start
  32.9 4.3 collective-permute-start
  48.8 4.3 collective-permute-start
  64.8 4.3 collective-permute-start
  80.7 4.3 collective-permute-start
  96.6 4.3 collective-permute-start
  112.6 4.3 collective-permute-start
  128.5 4.3 collective-permute-start
  144.4 4.3 collective-permute-start
  160.4 4.3 collective-permute-start
  176.3 4.3 collective-permute-start
  192.2 4.3 collective-permute-start
  208.2 4.3 collective-permute-start
  224.1 4.3 collective-permute-start
  240.0 4.9 collective-permute-start
  256.6 6.4 collective-permute-start
  277.1 70.7 %all_to_all.16 = bf16[128,8,256]{0,2,1:T(8,128)(2,1)S(1)} all-to-all(bf16[128,8,256]{0,2,1:T(8,128)(2,1)S(1)} %bitcast.89), channel_id=1, replica_groups=mesh['dp'=8,'ctx'=16] {'dp'}, dimensions={1} | all-to-all | bytes 1048576 | tf_op jit(solution)/shard_map/all_to_all | solution.py:132
  348.0 5.6 convolution_convert_fusion.1
  353.7 119.3 %reduce-scatter.3.cloned.1.call-done = bf16[128,4096]{1,0:T(8,128)(2,1)} async-done(((bf16[1024,4096]{1,0:T(8,128)(2,1)}), bf16[128,4096]{1,0:T(8,128)(2,1)}) %reduce-scatter.3.cloned.1.call-update) | async-done | bytes 1048592 | tf_op jit(solution)/shard_map/reduce_scatter | solution.py:133
  477.5 106.7 %all-gather.2.cloned.1.call-done = bf16[1024,4096]{1,0:T(8,128)(2,1)} async-done(((bf16[128,4096]{1,0:T(8,128)(2,1)}), bf16[1024,4096]{1,0:T(8,128)(2,1)}) %all-gather.2.cloned.1.call-update) | async-done | bytes 8388624 | tf_op jit(solution)/shard_map/all_gather | solution.py:142
  584.2 14.6 %fusion.31 = f32[1024,896]{1,0:T(8,128)} fusion(bf16[1024,4096]{1,0:T(8,128)(2,1)} %all-gather.2.cloned.1.call-done, bf16[4096,896]{1,0:T(8,128)(2,1)} %param.19), kind=kOutput, calls=%fused_computation.67 | convolution fusion | flops 7516192768 | bytes 19398656 | tf_op jit(solution)/shard_map/dot_general | solution.py:143
  598.8 26.7 %convolution_convert_fusion = bf16[1024,4096]{1,0:T(8,128)(2,1)} fusion(bf16[896,4096]{1,0:T(8,128)(2,1)} %param.21, f32[1024,896]{1,0:T(8,128)} %fusion.31, bf16[1024,4096]{1,0:T(8,128)(2,1)} %all-gather.2.cloned.1.call-done, bf16[4096,896]{1,0:T(8,128)(2,1)} %param.20), kind=kOutput, calls=%fused_computation.20 | convolution fusion | flops 15042084864 | bytes 35127296 | tf_op jit(solution)/shard_map/dot_general | solution.py:146
  625.6 112.7 %reduce-scatter.5.cloned.1.call-done = bf16[128,4096]{1,0:T(8,128)(2,1)} async-done(((bf16[1024,4096]{1,0:T(8,128)(2,1)}), bf16[128,4096]{1,0:T(8,128)(2,1)}) %reduce-scatter.5.cloned.1.call-update) | async-done | bytes 1048592 | tf_op jit(solution)/shard_map/reduce_scatter | solution.py:147
  (314 shorter events, 205.4 us)
Async XLA Ops:
  6.5 341.5 %copy-start = (bf16[256,4096]{1,0:T(8,128)(2,1)S(1)}, bf16[256,4096]{1,0:T(8,128)(2,1)}, u32[]{:S(2)}) copy-start(bf16[256,4096]{1,0:T(8,128)(2,1)} %param.17) | copy-start | bytes 6291460
  6.5 466.5 %reduce-scatter.3.cloned.1.call-start = ((), (), s32[]{:S(2)}) async-start(), calls=%async_computation.3 | async-start | bytes 9437184 | tf_op jit(solution)/shard_map/reduce_scatter | solution.py:133
  14.1 1.8 copy-start.5
  16.7 8.2 %collective-permute-start = (bf16[2,128,512]{1,2,0:T(8,128)(2,1)}, bf16[2,128,512]{1,2,0:T(8,128)(2,1)S(1)}, u32[]{:S(2)}, u32[]{:S(2)}) collective-permute-start(bf16[2,128,512]{1,2,0:T(8,128)(2,1)} %get-tuple-element.391), channel_id=1, source_target_pairs={{0,1},{1,2},{2,3},{3,4},{4,5},{5,6},{6,7},{7,8},{8,9},{9,10},{10,1... | collective-permute-start | bytes 786440 | tf_op jit(solution)/shard_map/while/body/eval_jaxpr/ppermute | solution.py:16
  32.9 7.9 %collective-permute-start = (bf16[2,128,512]{1,2,0:T(8,128)(2,1)}, bf16[2,128,512]{1,2,0:T(8,128)(2,1)S(1)}, u32[]{:S(2)}, u32[]{:S(2)}) collective-permute-start(bf16[2,128,512]{1,2,0:T(8,128)(2,1)} %get-tuple-element.391), channel_id=1, source_target_pairs={{0,1},{1,2},{2,3},{3,4},{4,5},{5,6},{6,7},{7,8},{8,9},{9,10},{10,1... | collective-permute-start | bytes 786440 | tf_op jit(solution)/shard_map/while/body/eval_jaxpr/ppermute | solution.py:16
  48.8 7.9 %collective-permute-start = (bf16[2,128,512]{1,2,0:T(8,128)(2,1)}, bf16[2,128,512]{1,2,0:T(8,128)(2,1)S(1)}, u32[]{:S(2)}, u32[]{:S(2)}) collective-permute-start(bf16[2,128,512]{1,2,0:T(8,128)(2,1)} %get-tuple-element.391), channel_id=1, source_target_pairs={{0,1},{1,2},{2,3},{3,4},{4,5},{5,6},{6,7},{7,8},{8,9},{9,10},{10,1... | collective-permute-start | bytes 786440 | tf_op jit(solution)/shard_map/while/body/eval_jaxpr/ppermute | solution.py:16
  64.8 7.9 %collective-permute-start = (bf16[2,128,512]{1,2,0:T(8,128)(2,1)}, bf16[2,128,512]{1,2,0:T(8,128)(2,1)S(1)}, u32[]{:S(2)}, u32[]{:S(2)}) collective-permute-start(bf16[2,128,512]{1,2,0:T(8,128)(2,1)} %get-tuple-element.391), channel_id=1, source_target_pairs={{0,1},{1,2},{2,3},{3,4},{4,5},{5,6},{6,7},{7,8},{8,9},{9,10},{10,1... | collective-permute-start | bytes 786440 | tf_op jit(solution)/shard_map/while/body/eval_jaxpr/ppermute | solution.py:16
  80.7 7.9 %collective-permute-start = (bf16[2,128,512]{1,2,0:T(8,128)(2,1)}, bf16[2,128,512]{1,2,0:T(8,128)(2,1)S(1)}, u32[]{:S(2)}, u32[]{:S(2)}) collective-permute-start(bf16[2,128,512]{1,2,0:T(8,128)(2,1)} %get-tuple-element.391), channel_id=1, source_target_pairs={{0,1},{1,2},{2,3},{3,4},{4,5},{5,6},{6,7},{7,8},{8,9},{9,10},{10,1... | collective-permute-start | bytes 786440 | tf_op jit(solution)/shard_map/while/body/eval_jaxpr/ppermute | solution.py:16
  96.6 7.9 %collective-permute-start = (bf16[2,128,512]{1,2,0:T(8,128)(2,1)}, bf16[2,128,512]{1,2,0:T(8,128)(2,1)S(1)}, u32[]{:S(2)}, u32[]{:S(2)}) collective-permute-start(bf16[2,128,512]{1,2,0:T(8,128)(2,1)} %get-tuple-element.391), channel_id=1, source_target_pairs={{0,1},{1,2},{2,3},{3,4},{4,5},{5,6},{6,7},{7,8},{8,9},{9,10},{10,1... | collective-permute-start | bytes 786440 | tf_op jit(solution)/shard_map/while/body/eval_jaxpr/ppermute | solution.py:16
  112.6 7.9 %collective-permute-start = (bf16[2,128,512]{1,2,0:T(8,128)(2,1)}, bf16[2,128,512]{1,2,0:T(8,128)(2,1)S(1)}, u32[]{:S(2)}, u32[]{:S(2)}) collective-permute-start(bf16[2,128,512]{1,2,0:T(8,128)(2,1)} %get-tuple-element.391), channel_id=1, source_target_pairs={{0,1},{1,2},{2,3},{3,4},{4,5},{5,6},{6,7},{7,8},{8,9},{9,10},{10,1... | collective-permute-start | bytes 786440 | tf_op jit(solution)/shard_map/while/body/eval_jaxpr/ppermute | solution.py:16
  128.5 7.9 %collective-permute-start = (bf16[2,128,512]{1,2,0:T(8,128)(2,1)}, bf16[2,128,512]{1,2,0:T(8,128)(2,1)S(1)}, u32[]{:S(2)}, u32[]{:S(2)}) collective-permute-start(bf16[2,128,512]{1,2,0:T(8,128)(2,1)} %get-tuple-element.391), channel_id=1, source_target_pairs={{0,1},{1,2},{2,3},{3,4},{4,5},{5,6},{6,7},{7,8},{8,9},{9,10},{10,1... | collective-permute-start | bytes 786440 | tf_op jit(solution)/shard_map/while/body/eval_jaxpr/ppermute | solution.py:16
  144.4 7.9 %collective-permute-start = (bf16[2,128,512]{1,2,0:T(8,128)(2,1)}, bf16[2,128,512]{1,2,0:T(8,128)(2,1)S(1)}, u32[]{:S(2)}, u32[]{:S(2)}) collective-permute-start(bf16[2,128,512]{1,2,0:T(8,128)(2,1)} %get-tuple-element.391), channel_id=1, source_target_pairs={{0,1},{1,2},{2,3},{3,4},{4,5},{5,6},{6,7},{7,8},{8,9},{9,10},{10,1... | collective-permute-start | bytes 786440 | tf_op jit(solution)/shard_map/while/body/eval_jaxpr/ppermute | solution.py:16
  160.4 7.9 %collective-permute-start = (bf16[2,128,512]{1,2,0:T(8,128)(2,1)}, bf16[2,128,512]{1,2,0:T(8,128)(2,1)S(1)}, u32[]{:S(2)}, u32[]{:S(2)}) collective-permute-start(bf16[2,128,512]{1,2,0:T(8,128)(2,1)} %get-tuple-element.391), channel_id=1, source_target_pairs={{0,1},{1,2},{2,3},{3,4},{4,5},{5,6},{6,7},{7,8},{8,9},{9,10},{10,1... | collective-permute-start | bytes 786440 | tf_op jit(solution)/shard_map/while/body/eval_jaxpr/ppermute | solution.py:16
  176.3 7.9 %collective-permute-start = (bf16[2,128,512]{1,2,0:T(8,128)(2,1)}, bf16[2,128,512]{1,2,0:T(8,128)(2,1)S(1)}, u32[]{:S(2)}, u32[]{:S(2)}) collective-permute-start(bf16[2,128,512]{1,2,0:T(8,128)(2,1)} %get-tuple-element.391), channel_id=1, source_target_pairs={{0,1},{1,2},{2,3},{3,4},{4,5},{5,6},{6,7},{7,8},{8,9},{9,10},{10,1... | collective-permute-start | bytes 786440 | tf_op jit(solution)/shard_map/while/body/eval_jaxpr/ppermute | solution.py:16
  192.2 7.9 %collective-permute-start = (bf16[2,128,512]{1,2,0:T(8,128)(2,1)}, bf16[2,128,512]{1,2,0:T(8,128)(2,1)S(1)}, u32[]{:S(2)}, u32[]{:S(2)}) collective-permute-start(bf16[2,128,512]{1,2,0:T(8,128)(2,1)} %get-tuple-element.391), channel_id=1, source_target_pairs={{0,1},{1,2},{2,3},{3,4},{4,5},{5,6},{6,7},{7,8},{8,9},{9,10},{10,1... | collective-permute-start | bytes 786440 | tf_op jit(solution)/shard_map/while/body/eval_jaxpr/ppermute | solution.py:16
  208.2 7.9 %collective-permute-start = (bf16[2,128,512]{1,2,0:T(8,128)(2,1)}, bf16[2,128,512]{1,2,0:T(8,128)(2,1)S(1)}, u32[]{:S(2)}, u32[]{:S(2)}) collective-permute-start(bf16[2,128,512]{1,2,0:T(8,128)(2,1)} %get-tuple-element.391), channel_id=1, source_target_pairs={{0,1},{1,2},{2,3},{3,4},{4,5},{5,6},{6,7},{7,8},{8,9},{9,10},{10,1... | collective-permute-start | bytes 786440 | tf_op jit(solution)/shard_map/while/body/eval_jaxpr/ppermute | solution.py:16
  224.1 7.9 %collective-permute-start = (bf16[2,128,512]{1,2,0:T(8,128)(2,1)}, bf16[2,128,512]{1,2,0:T(8,128)(2,1)S(1)}, u32[]{:S(2)}, u32[]{:S(2)}) collective-permute-start(bf16[2,128,512]{1,2,0:T(8,128)(2,1)} %get-tuple-element.391), channel_id=1, source_target_pairs={{0,1},{1,2},{2,3},{3,4},{4,5},{5,6},{6,7},{7,8},{8,9},{9,10},{10,1... | collective-permute-start | bytes 786440 | tf_op jit(solution)/shard_map/while/body/eval_jaxpr/ppermute | solution.py:16
  240.0 8.5 %collective-permute-start = (bf16[2,128,512]{1,2,0:T(8,128)(2,1)}, bf16[2,128,512]{1,2,0:T(8,128)(2,1)S(1)}, u32[]{:S(2)}, u32[]{:S(2)}) collective-permute-start(bf16[2,128,512]{1,2,0:T(8,128)(2,1)} %get-tuple-element.391), channel_id=1, source_target_pairs={{0,1},{1,2},{2,3},{3,4},{4,5},{5,6},{6,7},{7,8},{8,9},{9,10},{10,1... | collective-permute-start | bytes 786440 | tf_op jit(solution)/shard_map/while/body/eval_jaxpr/ppermute | solution.py:16
  256.6 10.0 %collective-permute-start = (bf16[2,128,512]{1,2,0:T(8,128)(2,1)}, bf16[2,128,512]{1,2,0:T(8,128)(2,1)S(1)}, u32[]{:S(2)}, u32[]{:S(2)}) collective-permute-start(bf16[2,128,512]{1,2,0:T(8,128)(2,1)} %get-tuple-element.391), channel_id=1, source_target_pairs={{0,1},{1,2},{2,3},{3,4},{4,5},{5,6},{6,7},{7,8},{8,9},{9,10},{10,1... | collective-permute-start | bytes 786440 | tf_op jit(solution)/shard_map/while/body/eval_jaxpr/ppermute | solution.py:16
  353.6 119.4 %copy-start.3 = (bf16[128,4096]{1,0:T(8,128)(2,1)S(1)}, bf16[128,4096]{1,0:T(8,128)(2,1)}, u32[]{:S(2)}) copy-start(bf16[128,4096]{1,0:T(8,128)(2,1)} %param.12) | copy-start | bytes 3145732
  353.6 121.1 %copy-start.6 = (f32[4096]{0:T(1024)S(1)}, f32[4096]{0:T(1024)}, u32[]{:S(2)}) copy-start(f32[4096]{0:T(1024)} %param.18) | copy-start | bytes 49156
  353.6 230.6 %all-gather.2.cloned.1.call-start = ((), (), s32[]{:S(2)}) async-start(), calls=%async_computation.4 | async-start | bytes 9437184 | tf_op jit(solution)/shard_map/all_gather | solution.py:142
  477.3 261.0 %reduce-scatter.5.cloned.1.call-start = ((), (), s32[]{:S(2)}) async-start(), calls=%async_computation.5 | async-start | bytes 9437184 | tf_op jit(solution)/shard_map/reduce_scatter | solution.py:147
  625.5 115.7 %copy-start.1 = (bf16[256,4096]{1,0:T(8,128)(2,1)S(1)}, bf16[256,4096]{1,0:T(8,128)(2,1)}, u32[]{:S(2)}) copy-start(bf16[256,4096]{1,0:T(8,128)(2,1)} %param.17) | copy-start | bytes 6291460
  (2 other events, 2.6 us)
Sparse Core Ops, SparseCore 0:
  353.8 119.2 reduce-scatter.2
  477.4 106.7 all-gather.1
  625.7 112.5 reduce-scatter.4
where the time goes:
time: 750 us; the launch traced here: 748 us
  waiting for transfers between devices  393 us (52%)
  matrix products  96.2 us (13%)
  local copies, waits for them, and re-layouts  83.5 us (11%)
  starting transfers between devices  71.7 us (10%)
  blocking collectives  70.7 us (9%)
  other arithmetic  18.2 us (2%)
  between operations  13.3 us (2%)
    reduce_scatter x1, waiting for transfers between devices, per_device(): lax.psum_scatter(jnp.dot(spread, w_out, preferred_element_type=jnp.float3...  119 us
    reduce_scatter x1, waiting for transfers between devices, per_device(): lax.psum_scatter(partial_rows.astype(jnp.bfloat16), 'dp', scatter_dimensi...  113 us
    all_gather x1, waiting for transfers between devices, per_device(): piece_rows = lax.all_gather(normed, 'dp', axis=0, tiled=True)  107 us
    ppermute x16, starting transfers between devices, from_behind(): return lax.ppermute(block, axis, route)  71.4 us
    all_to_all x1, blocking collectives, per_device(): lax.all_to_all(heads_out, 'dp', split_axis=1, concat_axis=0, tiled=True)  70.7 us
    ppermute x16, waiting for transfers between devices, from_behind(): return lax.ppermute(block, axis, route)  54 us
    dot_general x1, matrix products, per_device(): jnp.dot(hidden_act, w_down, preferred_element_type=jnp.float32)  26.7 us
    squeeze x16, local copies, waits for them, and re-layouts, online_update(): value_rows.reshape(value_rows.shape[0], kv_heads, head_dim)  26.7 us
  transfers between devices with their start and end apart: 19, of which 19 were waited for; matrix products, arithmetic and copies ran while one was open for 0% of the time, Pallas kernels for 0%

commit v1 on v0

--- a/solution.py
+++ b/solution.py
@@ -129,7 +129,10 @@
     heads_out = (
         heads_out.transpose(2, 0, 1, 3).reshape(tok_rows, num_heads * head_dim).astype(jnp.bfloat16)
     )
-    spread = lax.all_to_all(heads_out, "dp", split_axis=1, concat_axis=0, tiled=True)
+    size = lax.axis_size("dp")
+    tiles = jnp.stack(jnp.split(heads_out, size, axis=1), axis=0)
+    tiles = lax.all_to_all(tiles, "dp", split_axis=0, concat_axis=0)
+    spread = jnp.concatenate(tiles, axis=0)
     projected = lax.psum_scatter(
         jnp.dot(spread, w_out, preferred_element_type=jnp.float32).astype(jnp.bfloat16),
         "dp",

time: 750 us -> 750 us (level)
  no operation moved by 1% of the time
where the time goes in v1:
time: 750 us; the launch traced here: 748 us
  waiting for transfers between devices  393 us (52%)
  matrix products  96.2 us (13%)
  local copies, waits for them, and re-layouts  83.7 us (11%)
  starting transfers between devices  71.7 us (10%)
  blocking collectives  70.7 us (9%)
  other arithmetic  18.2 us (2%)
  between operations  13.4 us (2%)
    reduce_scatter x1, waiting for transfers between devices, per_device(): lax.psum_scatter(jnp.dot(spread, w_out, preferred_element_type=jnp.float3...  119 us
    reduce_scatter x1, waiting for transfers between devices, per_device(): lax.psum_scatter(partial_rows.astype(jnp.bfloat16), 'dp', scatter_dimensi...  113 us
    all_gather x1, waiting for transfers between devices, per_device(): piece_rows = lax.all_gather(normed, 'dp', axis=0, tiled=True)  107 us
    ppermute x16, starting transfers between devices, from_behind(): return lax.ppermute(block, axis, route)  71.4 us
    all_to_all x1, blocking collectives, per_device(): tiles = lax.all_to_all(tiles, 'dp', split_axis=0, concat_axis=0)  70.7 us
    ppermute x16, waiting for transfers between devices, from_behind(): return lax.ppermute(block, axis, route)  54 us
    dot_general x1, matrix products, per_device(): jnp.dot(hidden_act, w_down, preferred_element_type=jnp.float32)  26.7 us
    squeeze x16, local copies, waits for them, and re-layouts, online_update(): value_rows.reshape(value_rows.shape[0], kv_heads, head_dim)  26.7 us
  transfers between devices with their start and end apart: 19, of which 19 were waited for; matrix products, arithmetic and copies ran while one was open for 0% of the time, Pallas kernels for 0%

profile of v1, /device:TPU:1, one launch (start us, length us, event | category | flops | bytes accessed | tf_op | source)
XLA Modules:
  0.0 748.2 jit_solution(8058963935906549876)
XLA Ops:
  16.7 258.0 %while.22 = (s32[]{:T(128)}, f32[4,512]{1,0:T(4,128)S(1)}, f32[4,512]{1,0:T(4,128)S(1)}, f32[4,512,128]{2,1,0:T(8,128)S(1)}, bf16[2,128,512]{1,2,0:T(8,128)(2,1)...) while((s32[]{:T(128)}, f32[4,512]{1,0:T(4,128)S(1)}, ...), condition=%wide.region_7.8_spmd.clone, body=%wide.region_4.7_spmd.clone.sunk | while | flops 137154816 | bytes 9210569 | solution.py:126
  16.7 4.6 collective-permute-start
  32.9 4.3 collective-permute-start
  48.8 4.3 collective-permute-start
  64.8 4.3 collective-permute-start
  80.7 4.3 collective-permute-start
  96.6 4.3 collective-permute-start
  112.6 4.3 collective-permute-start
  128.5 4.3 collective-permute-start
  144.4 4.3 collective-permute-start
  160.4 4.3 collective-permute-start
  176.3 4.3 collective-permute-start
  192.2 4.3 collective-permute-start
  208.2 4.3 collective-permute-start
  224.1 4.3 collective-permute-start
  240.0 4.9 collective-permute-start
  256.6 6.4 collective-permute-start
  277.2 70.7 %all_to_all.5 = bf16[8,128,256]{1,2,0:T(8,128)(2,1)S(1)} all-to-all(bf16[8,128,256]{1,2,0:T(8,128)(2,1)S(1)} %fusion.24), channel_id=1, replica_groups=mesh['dp'=8,'ctx'=16] {'dp'}, dimensions={0} | all-to-all | bytes 1048576 | tf_op jit(solution)/shard_map/all_to_all | solution.py:134
  348.2 5.6 convolution_convert_fusion.1
  353.8 119.4 %reduce-scatter.3.cloned.1.call-done = bf16[128,4096]{1,0:T(8,128)(2,1)} async-done(((bf16[1024,4096]{1,0:T(8,128)(2,1)}), bf16[128,4096]{1,0:T(8,128)(2,1)}) %reduce-scatter.3.cloned.1.call-update) | async-done | bytes 1048592 | tf_op jit(solution)/shard_map/reduce_scatter | solution.py:136
  477.7 106.7 %all-gather.2.cloned.1.call-done = bf16[1024,4096]{1,0:T(8,128)(2,1)} async-done(((bf16[128,4096]{1,0:T(8,128)(2,1)}), bf16[1024,4096]{1,0:T(8,128)(2,1)}) %all-gather.2.cloned.1.call-update) | async-done | bytes 8388624 | tf_op jit(solution)/shard_map/all_gather | solution.py:145
  584.4 14.6 %fusion.39 = f32[1024,896]{1,0:T(8,128)} fusion(bf16[1024,4096]{1,0:T(8,128)(2,1)} %all-gather.2.cloned.1.call-done, bf16[4096,896]{1,0:T(8,128)(2,1)} %param.19), kind=kOutput, calls=%fused_computation.83 | convolution fusion | flops 7516192768 | bytes 19398656 | tf_op jit(solution)/shard_map/dot_general | solution.py:146
  599.0 26.7 %convolution_convert_fusion = bf16[1024,4096]{1,0:T(8,128)(2,1)} fusion(bf16[896,4096]{1,0:T(8,128)(2,1)} %param.21, f32[1024,896]{1,0:T(8,128)} %fusion.39, bf16[1024,4096]{1,0:T(8,128)(2,1)} %all-gather.2.cloned.1.call-done, bf16[4096,896]{1,0:T(8,128)(2,1)} %param.20), kind=kOutput, calls=%fused_computation.20 | convolution fusion | flops 15042084864 | bytes 35127296 | tf_op jit(solution)/shard_map/dot_general | solution.py:149
  625.8 112.9 %reduce-scatter.5.cloned.1.call-done = bf16[128,4096]{1,0:T(8,128)(2,1)} async-done(((bf16[1024,4096]{1,0:T(8,128)(2,1)}), bf16[128,4096]{1,0:T(8,128)(2,1)}) %reduce-scatter.5.cloned.1.call-update) | async-done | bytes 1048592 | tf_op jit(solution)/shard_map/reduce_scatter | solution.py:150
  (322 shorter events, 205.5 us)
Async XLA Ops:
  6.5 341.6 %copy-start = (bf16[256,4096]{1,0:T(8,128)(2,1)S(1)}, bf16[256,4096]{1,0:T(8,128)(2,1)}, u32[]{:S(2)}) copy-start(bf16[256,4096]{1,0:T(8,128)(2,1)} %param.17) | copy-start | bytes 6291460
  6.5 466.7 %reduce-scatter.3.cloned.1.call-start = ((), (), s32[]{:S(2)}) async-start(), calls=%async_computation.3 | async-start | bytes 9437184 | tf_op jit(solution)/shard_map/reduce_scatter | solution.py:136
  14.1 1.8 copy-start.5
  16.7 8.2 %collective-permute-start = (bf16[2,128,512]{1,2,0:T(8,128)(2,1)}, bf16[2,128,512]{1,2,0:T(8,128)(2,1)S(1)}, u32[]{:S(2)}, u32[]{:S(2)}) collective-permute-start(bf16[2,128,512]{1,2,0:T(8,128)(2,1)} %get-tuple-element.391), channel_id=1, source_target_pairs={{0,1},{1,2},{2,3},{3,4},{4,5},{5,6},{6,7},{7,8},{8,9},{9,10},{10,1... | collective-permute-start | bytes 786440 | tf_op jit(solution)/shard_map/while/body/eval_jaxpr/ppermute | solution.py:16
  32.9 7.9 %collective-permute-start = (bf16[2,128,512]{1,2,0:T(8,128)(2,1)}, bf16[2,128,512]{1,2,0:T(8,128)(2,1)S(1)}, u32[]{:S(2)}, u32[]{:S(2)}) collective-permute-start(bf16[2,128,512]{1,2,0:T(8,128)(2,1)} %get-tuple-element.391), channel_id=1, source_target_pairs={{0,1},{1,2},{2,3},{3,4},{4,5},{5,6},{6,7},{7,8},{8,9},{9,10},{10,1... | collective-permute-start | bytes 786440 | tf_op jit(solution)/shard_map/while/body/eval_jaxpr/ppermute | solution.py:16
  48.8 7.9 %collective-permute-start = (bf16[2,128,512]{1,2,0:T(8,128)(2,1)}, bf16[2,128,512]{1,2,0:T(8,128)(2,1)S(1)}, u32[]{:S(2)}, u32[]{:S(2)}) collective-permute-start(bf16[2,128,512]{1,2,0:T(8,128)(2,1)} %get-tuple-element.391), channel_id=1, source_target_pairs={{0,1},{1,2},{2,3},{3,4},{4,5},{5,6},{6,7},{7,8},{8,9},{9,10},{10,1... | collective-permute-start | bytes 786440 | tf_op jit(solution)/shard_map/while/body/eval_jaxpr/ppermute | solution.py:16
  64.8 7.9 %collective-permute-start = (bf16[2,128,512]{1,2,0:T(8,128)(2,1)}, bf16[2,128,512]{1,2,0:T(8,128)(2,1)S(1)}, u32[]{:S(2)}, u32[]{:S(2)}) collective-permute-start(bf16[2,128,512]{1,2,0:T(8,128)(2,1)} %get-tuple-element.391), channel_id=1, source_target_pairs={{0,1},{1,2},{2,3},{3,4},{4,5},{5,6},{6,7},{7,8},{8,9},{9,10},{10,1... | collective-permute-start | bytes 786440 | tf_op jit(solution)/shard_map/while/body/eval_jaxpr/ppermute | solution.py:16
  80.7 7.9 %collective-permute-start = (bf16[2,128,512]{1,2,0:T(8,128)(2,1)}, bf16[2,128,512]{1,2,0:T(8,128)(2,1)S(1)}, u32[]{:S(2)}, u32[]{:S(2)}) collective-permute-start(bf16[2,128,512]{1,2,0:T(8,128)(2,1)} %get-tuple-element.391), channel_id=1, source_target_pairs={{0,1},{1,2},{2,3},{3,4},{4,5},{5,6},{6,7},{7,8},{8,9},{9,10},{10,1... | collective-permute-start | bytes 786440 | tf_op jit(solution)/shard_map/while/body/eval_jaxpr/ppermute | solution.py:16
  96.6 7.9 %collective-permute-start = (bf16[2,128,512]{1,2,0:T(8,128)(2,1)}, bf16[2,128,512]{1,2,0:T(8,128)(2,1)S(1)}, u32[]{:S(2)}, u32[]{:S(2)}) collective-permute-start(bf16[2,128,512]{1,2,0:T(8,128)(2,1)} %get-tuple-element.391), channel_id=1, source_target_pairs={{0,1},{1,2},{2,3},{3,4},{4,5},{5,6},{6,7},{7,8},{8,9},{9,10},{10,1... | collective-permute-start | bytes 786440 | tf_op jit(solution)/shard_map/while/body/eval_jaxpr/ppermute | solution.py:16
  112.6 7.9 %collective-permute-start = (bf16[2,128,512]{1,2,0:T(8,128)(2,1)}, bf16[2,128,512]{1,2,0:T(8,128)(2,1)S(1)}, u32[]{:S(2)}, u32[]{:S(2)}) collective-permute-start(bf16[2,128,512]{1,2,0:T(8,128)(2,1)} %get-tuple-element.391), channel_id=1, source_target_pairs={{0,1},{1,2},{2,3},{3,4},{4,5},{5,6},{6,7},{7,8},{8,9},{9,10},{10,1... | collective-permute-start | bytes 786440 | tf_op jit(solution)/shard_map/while/body/eval_jaxpr/ppermute | solution.py:16
  128.5 7.9 %collective-permute-start = (bf16[2,128,512]{1,2,0:T(8,128)(2,1)}, bf16[2,128,512]{1,2,0:T(8,128)(2,1)S(1)}, u32[]{:S(2)}, u32[]{:S(2)}) collective-permute-start(bf16[2,128,512]{1,2,0:T(8,128)(2,1)} %get-tuple-element.391), channel_id=1, source_target_pairs={{0,1},{1,2},{2,3},{3,4},{4,5},{5,6},{6,7},{7,8},{8,9},{9,10},{10,1... | collective-permute-start | bytes 786440 | tf_op jit(solution)/shard_map/while/body/eval_jaxpr/ppermute | solution.py:16
  144.4 7.9 %collective-permute-start = (bf16[2,128,512]{1,2,0:T(8,128)(2,1)}, bf16[2,128,512]{1,2,0:T(8,128)(2,1)S(1)}, u32[]{:S(2)}, u32[]{:S(2)}) collective-permute-start(bf16[2,128,512]{1,2,0:T(8,128)(2,1)} %get-tuple-element.391), channel_id=1, source_target_pairs={{0,1},{1,2},{2,3},{3,4},{4,5},{5,6},{6,7},{7,8},{8,9},{9,10},{10,1... | collective-permute-start | bytes 786440 | tf_op jit(solution)/shard_map/while/body/eval_jaxpr/ppermute | solution.py:16
  160.4 7.9 %collective-permute-start = (bf16[2,128,512]{1,2,0:T(8,128)(2,1)}, bf16[2,128,512]{1,2,0:T(8,128)(2,1)S(1)}, u32[]{:S(2)}, u32[]{:S(2)}) collective-permute-start(bf16[2,128,512]{1,2,0:T(8,128)(2,1)} %get-tuple-element.391), channel_id=1, source_target_pairs={{0,1},{1,2},{2,3},{3,4},{4,5},{5,6},{6,7},{7,8},{8,9},{9,10},{10,1... | collective-permute-start | bytes 786440 | tf_op jit(solution)/shard_map/while/body/eval_jaxpr/ppermute | solution.py:16
  176.3 7.9 %collective-permute-start = (bf16[2,128,512]{1,2,0:T(8,128)(2,1)}, bf16[2,128,512]{1,2,0:T(8,128)(2,1)S(1)}, u32[]{:S(2)}, u32[]{:S(2)}) collective-permute-start(bf16[2,128,512]{1,2,0:T(8,128)(2,1)} %get-tuple-element.391), channel_id=1, source_target_pairs={{0,1},{1,2},{2,3},{3,4},{4,5},{5,6},{6,7},{7,8},{8,9},{9,10},{10,1... | collective-permute-start | bytes 786440 | tf_op jit(solution)/shard_map/while/body/eval_jaxpr/ppermute | solution.py:16
  192.2 7.9 %collective-permute-start = (bf16[2,128,512]{1,2,0:T(8,128)(2,1)}, bf16[2,128,512]{1,2,0:T(8,128)(2,1)S(1)}, u32[]{:S(2)}, u32[]{:S(2)}) collective-permute-start(bf16[2,128,512]{1,2,0:T(8,128)(2,1)} %get-tuple-element.391), channel_id=1, source_target_pairs={{0,1},{1,2},{2,3},{3,4},{4,5},{5,6},{6,7},{7,8},{8,9},{9,10},{10,1... | collective-permute-start | bytes 786440 | tf_op jit(solution)/shard_map/while/body/eval_jaxpr/ppermute | solution.py:16
  208.2 7.9 %collective-permute-start = (bf16[2,128,512]{1,2,0:T(8,128)(2,1)}, bf16[2,128,512]{1,2,0:T(8,128)(2,1)S(1)}, u32[]{:S(2)}, u32[]{:S(2)}) collective-permute-start(bf16[2,128,512]{1,2,0:T(8,128)(2,1)} %get-tuple-element.391), channel_id=1, source_target_pairs={{0,1},{1,2},{2,3},{3,4},{4,5},{5,6},{6,7},{7,8},{8,9},{9,10},{10,1... | collective-permute-start | bytes 786440 | tf_op jit(solution)/shard_map/while/body/eval_jaxpr/ppermute | solution.py:16
  224.1 7.9 %collective-permute-start = (bf16[2,128,512]{1,2,0:T(8,128)(2,1)}, bf16[2,128,512]{1,2,0:T(8,128)(2,1)S(1)}, u32[]{:S(2)}, u32[]{:S(2)}) collective-permute-start(bf16[2,128,512]{1,2,0:T(8,128)(2,1)} %get-tuple-element.391), channel_id=1, source_target_pairs={{0,1},{1,2},{2,3},{3,4},{4,5},{5,6},{6,7},{7,8},{8,9},{9,10},{10,1... | collective-permute-start | bytes 786440 | tf_op jit(solution)/shard_map/while/body/eval_jaxpr/ppermute | solution.py:16
  240.0 8.5 %collective-permute-start = (bf16[2,128,512]{1,2,0:T(8,128)(2,1)}, bf16[2,128,512]{1,2,0:T(8,128)(2,1)S(1)}, u32[]{:S(2)}, u32[]{:S(2)}) collective-permute-start(bf16[2,128,512]{1,2,0:T(8,128)(2,1)} %get-tuple-element.391), channel_id=1, source_target_pairs={{0,1},{1,2},{2,3},{3,4},{4,5},{5,6},{6,7},{7,8},{8,9},{9,10},{10,1... | collective-permute-start | bytes 786440 | tf_op jit(solution)/shard_map/while/body/eval_jaxpr/ppermute | solution.py:16
  256.6 10.0 %collective-permute-start = (bf16[2,128,512]{1,2,0:T(8,128)(2,1)}, bf16[2,128,512]{1,2,0:T(8,128)(2,1)S(1)}, u32[]{:S(2)}, u32[]{:S(2)}) collective-permute-start(bf16[2,128,512]{1,2,0:T(8,128)(2,1)} %get-tuple-element.391), channel_id=1, source_target_pairs={{0,1},{1,2},{2,3},{3,4},{4,5},{5,6},{6,7},{7,8},{8,9},{9,10},{10,1... | collective-permute-start | bytes 786440 | tf_op jit(solution)/shard_map/while/body/eval_jaxpr/ppermute | solution.py:16
  353.8 119.5 %copy-start.3 = (bf16[128,4096]{1,0:T(8,128)(2,1)S(1)}, bf16[128,4096]{1,0:T(8,128)(2,1)}, u32[]{:S(2)}) copy-start(bf16[128,4096]{1,0:T(8,128)(2,1)} %param.12) | copy-start | bytes 3145732
  353.8 121.1 %copy-start.6 = (f32[4096]{0:T(1024)S(1)}, f32[4096]{0:T(1024)}, u32[]{:S(2)}) copy-start(f32[4096]{0:T(1024)} %param.18) | copy-start | bytes 49156
  353.8 230.7 %all-gather.2.cloned.1.call-start = ((), (), s32[]{:S(2)}) async-start(), calls=%async_computation.4 | async-start | bytes 9437184 | tf_op jit(solution)/shard_map/all_gather | solution.py:145
  477.5 261.2 %reduce-scatter.5.cloned.1.call-start = ((), (), s32[]{:S(2)}) async-start(), calls=%async_computation.5 | async-start | bytes 9437184 | tf_op jit(solution)/shard_map/reduce_scatter | solution.py:150
  625.7 115.9 %copy-start.1 = (bf16[256,4096]{1,0:T(8,128)(2,1)S(1)}, bf16[256,4096]{1,0:T(8,128)(2,1)}, u32[]{:S(2)}) copy-start(bf16[256,4096]{1,0:T(8,128)(2,1)} %param.17) | copy-start | bytes 6291460
  (2 other events, 2.6 us)
Sparse Core Ops, SparseCore 0:
  353.9 119.2 reduce-scatter.2
  477.6 106.7 all-gather.1
  625.9 112.7 reduce-scatter.4
